TPU v7x, 256 devices: a whole 4x4x8 slice. The times are simulated.
256 devices in a mesh: row: 32 (over y, z), col: 8 (over x, core).
Axes of the slice: x: 4, y: 4, z: 8, core: 2. Of those that a mesh axis runs over, the one named last changes fastest.
Arguments:
- panel: float32 [8, 32, 256, 256], P(None, 'row', None, 'col'), may hold values from -0.1875 to 0.1875
- slab: bfloat16 [8, 32, 256, 4, 8, 256], P(None, 'row', None, None, 'col'), may hold values from -6 to 6
- cotangent: bfloat16 [8, 32, 256, 4, 8, 256], P(None, 'row', None, None, 'col'), may hold values from -0.0625 to 0.0625
- inverse: float32 [256, 256], replicated, may hold values from -2 to 8, as said below
Outputs:
- updated: bfloat16 [8, 32, 256, 4, 8, 256], P(None, 'row', None, None, 'col')
- grad_panel: float32 [8, 32, 256, 256], P(None, 'row', None, 'col')
- grad_inverse: float32 [256, 256], P(None, 'col')
Inputs may be any that keep to these rules, and one draw needn't show every extreme that they name: `inverse`: lower triangular; diagonal entries between 4 and 8.
All inputs are finite; a program needn't handle non-finite values.
Results may differ from a plain program's by a relative error of at most 0.015.
Values may be sent and summed in bfloat16 or wider, within the bound.
A program may use at most 128 MiB of HBM per device.

v0:
```python
import jax
import jax.numpy as jnp
from jax import lax
from jax.sharding import PartitionSpec as P


def per_device(panel, slab, cotangent, inverse):
    tiles_local = panel.shape[0]
    tile_size = panel.shape[2]
    strip_width = panel.shape[3]
    slab_tiles = slab.shape[3]
    row_count = tiles_local * tile_size
    slab_width = slab_tiles * tile_size
    row_devices = lax.axis_size("row")
    col_devices = lax.axis_size("col")
    row_index = lax.axis_index("row")
    col_index = lax.axis_index("col")
    highest = lax.Precision.HIGHEST
    contract_rows = (((0,), (0,)), ((), ()))
    panel_rows = panel.reshape(row_count, strip_width)
    gathered = lax.all_gather(panel_rows, "col", axis=1, tiled=True)
    factor = jnp.dot(gathered, inverse.T, precision=highest, preferred_element_type=jnp.float32)
    rounded = factor.astype(jnp.bfloat16)
    factor_tiles = rounded.reshape(tiles_local, tile_size, tile_size)
    tile_list = []
    for column_slot in range(slab_tiles):
        tile_index = column_slot * col_devices + col_index
        is_owner = tile_index % row_devices == row_index
        owned_tile = lax.dynamic_index_in_dim(
            factor_tiles, tile_index // row_devices, 0, keepdims=False
        )
        tile_list.append(jnp.where(is_owner, owned_tile, jnp.zeros_like(owned_tile)))
    stacked = jnp.stack(tile_list).reshape(slab_width, tile_size)
    slab_factor = lax.psum(stacked, "row").astype(jnp.float32).astype(jnp.bfloat16)
    slab_rows = slab.reshape(row_count, slab_width)
    product = jnp.dot(rounded, slab_factor.T, preferred_element_type=jnp.float32)
    updated = (slab_rows.astype(jnp.float32) - product).astype(jnp.bfloat16)
    cot_rows = cotangent.reshape(row_count, slab_width)
    factor_grad = -jnp.dot(cot_rows, slab_factor, preferred_element_type=jnp.float32)
    slab_grad = -lax.dot_general(
        cot_rows, rounded, contract_rows, preferred_element_type=jnp.float32
    )
    slab_grad = lax.psum(slab_grad.astype(jnp.bfloat16), "row").astype(jnp.float32)
    grad_tiles = factor_grad.reshape(tiles_local, tile_size, tile_size)
    for column_slot in range(slab_tiles):
        tile_index = column_slot * col_devices + col_index
        is_owner = tile_index % row_devices == row_index
        local_slot = tile_index // row_devices
        current_tile = lax.dynamic_index_in_dim(grad_tiles, local_slot, 0, keepdims=True)
        added_tile = jnp.where(
            is_owner, slab_grad[column_slot * tile_size : (column_slot + 1) * tile_size], 0.0
        )
        grad_tiles = lax.dynamic_update_index_in_dim(
            grad_tiles, current_tile + added_tile[None], local_slot, 0
        )
    factor_grad = grad_tiles.reshape(row_count, tile_size)
    grad_total = lax.psum(factor_grad, "col")
    inverse_strip = lax.dynamic_slice_in_dim(inverse, col_index * strip_width, strip_width, 1)
    grad_panel = jnp.dot(
        grad_total, inverse_strip, precision=highest, preferred_element_type=jnp.float32
    )
    inverse_term = lax.dot_general(
        grad_total, panel_rows, contract_rows, precision=highest, preferred_element_type=jnp.float32
    )
    grad_inverse = lax.psum(inverse_term, "row")
    return (updated.reshape(slab.shape), grad_panel.reshape(panel.shape), grad_inverse)


def solution(mesh):
    in_specs = (
        P(None, "row", None, "col"),
        P(None, "row", None, None, "col", None),
        P(None, "row", None, None, "col", None),
        P(),
    )
    out_specs = (
        P(None, "row", None, None, "col", None),
        P(None, "row", None, "col"),
        P(None, "col"),
    )
    return jax.shard_map(
        per_device, mesh=mesh, in_specs=in_specs, out_specs=out_specs, check_vma=False
    )
```

profile of v0, /device:TPU:0, one launch (start us, length us, event | category | flops | bytes accessed | tf_op | source)
XLA Modules:
  0.0 430.0 jit_solution(7106329265095890)
XLA Ops:
  7.2 1.7 copy.19
  9.1 5.2 %copy.20 = bf16[256,8,4,256]{3,1,2,0:T(8,128)(2,1)} copy(bf16[256,8,4,256]{3,2,1,0:T(4,128)(2,1)} %bitcast.71) | data formatting | bytes 8388608
  14.3 24.5 %all-gather.2.cloned.1.call-done = f32[2048,256]{0,1:T(8,128)} async-done(((f32[2048,32]{0,1:T(8,128)}), f32[2048,256]{0,1:T(8,128)}) %all-gather.2.cloned.1.call-update) | async-done | bytes 2097168 | tf_op jit(solution)/shard_map/all_gather | solution.py:21
  38.8 5.0 %convolution_convert_fusion = bf16[2048,256]{1,0:T(8,128)(2,1)S(1)} fusion(f32[2048,256]{0,1:T(8,128)} %all-gather.2.cloned.1.call-done, f32[256,256]{1,0:T(8,128)S(1)} %copy-done), kind=kOutput, calls=%fused_computation.2 | convolution fusion | flops 1611137024 | bytes 3407872 | tf_op jit(solution)/shard_map/dot_general | solution.py:22
  43.9 4.3 fusion.1
  48.2 0.9 pad_maximum_fusion
  49.1 0.2 all-reduce.4.cloned.1.call-start
  49.3 150.0 %all-reduce.6.cloned.1.call-done = (bf16[1024,256]{1,0:T(8,128)(2,1)}, bf16[1024,256]{0,1:T(8,128)(2,1)}) async-done(((bf16[1024,256]{1,0:T(8,128)(2,1)}, bf16[1024,256]{0,1:T(8,128)(2,1)}), (bf16[1024,256]{1,0:T(8,128)(2,1)}, bf16[1024,256]{0,1:T(8,128)(2,1)})) %all-reduce.6.cloned.1.call-update) | async-done | bytes 1048592 | tf_op jit(solution)/shard_map/psum | solution.py:34
  199.3 3.7 convolution_negate_fusion
  202.9 0.2 copy.24
  203.1 0.9 copy-done.4
  204.0 0.1 convert_element_type.29
  204.1 0.1 fusion.13
  204.2 0.1 fusion.7
  204.4 1.8 copy.14
  206.2 7.0 %copy.18 = f32[256,8,4,256]{3,1,2,0:T(8,128)} copy(bf16[256,8,4,256]{3,2,1,0:T(4,128)(2,1)} %bitcast.70) | data formatting | bytes 12582912
  213.2 6.8 %subtract_convert_fusion = bf16[2048,1024]{1,0:T(8,128)(2,1)} fusion(f32[2048,1024]{1,0:T(8,128)} %bitcast.66, bf16[2048,256]{1,0:T(8,128)(2,1)S(1)} %convolution_convert_fusion, bf16[1024,256]{1,0:T(8,128)(2,1)S(1)} %copy-done.3), kind=kOutput, calls=%fused_computation | convolution fusion | flops 1077936128 | bytes 14155776 | tf_op jit(solution)/shard_map/dot_general | solution.py:36
  220.1 7.9 %reshape.36 = bf16[8,1,256,4,1,256]{5,3,2,0,4,1:T(4,128)(2,1)} reshape(bf16[2048,1024]{1,0:T(8,128)(2,1)} %subtract_convert_fusion) | data formatting | bytes 8388608 | tf_op jit(solution)/shard_map/reshape | solution.py:66
  227.9 46.6 %all-reduce.4.cloned.1.call-done = f32[2048,256]{1,0:T(8,128)} async-done(((f32[2048,256]{1,0:T(8,128)}), f32[2048,256]{1,0:T(8,128)}) %all-reduce.4.cloned.1.call-update) | async-done | bytes 2097168 | tf_op jit(solution)/shard_map/psum | solution.py:57
  274.5 3.8 fusion.14
  278.3 0.1 copy.21
  278.4 0.8 copy.16
  279.2 1.2 fusion.17
  280.4 143.1 %psum.31 = f32[256,32]{0,1:T(8,128)} all-reduce(f32[256,32]{0,1:T(8,128)S(1)} %fusion.17), channel_id=1, replica_groups=mesh['row'=32,'col'=8] {'row'}, use_global_device_ids=true, to_apply=%region_3.4 | all-reduce | flops 8192 | bytes 65536 | tf_op jit(solution)/shard_map/psum | solution.py:65
  (17 shorter events, 0.3 us)
Async XLA Ops:
  7.2 31.7 %copy-start = (f32[256,256]{1,0:T(8,128)S(1)}, f32[256,256]{1,0:T(8,128)}, u32[]{:S(2)}) copy-start(f32[256,256]{1,0:T(8,128)} %param.7) | copy-start | bytes 786436
  7.2 31.7 %all-gather.2.cloned.1.call-start = ((), (), s32[]{:S(2)}) async-start(), calls=%async_computation | async-start | bytes 2359296 | tf_op jit(solution)/shard_map/all_gather | solution.py:21
  9.0 190.3 %all-reduce.6.cloned.1.call-start = ((), (), s32[]{:S(2)}) async-start(), calls=%async_computation.2 | async-start | bytes 2097152 | tf_op jit(solution)/shard_map/psum | solution.py:34
  49.1 225.4 %all-reduce.4.cloned.1.call-start = ((), (), s32[]{:S(2)}) async-start(), calls=%async_computation.1 | async-start | bytes 4194304 | tf_op jit(solution)/shard_map/psum | solution.py:57
  202.9 1.0 copy-start.4
  206.2 7.0 %copy-start.3 = (bf16[1024,256]{1,0:T(8,128)(2,1)S(1)}, bf16[1024,256]{1,0:T(8,128)(2,1)}, u32[]{:S(2)}) copy-start(bf16[1024,256]{1,0:T(8,128)(2,1)} %get-tuple-element.9) | copy-start | bytes 1572868
  227.9 51.3 %copy-start.2 = (f32[4,8,8,256]{3,1,2,0:T(8,128)S(1)}, f32[4,8,8,256]{3,1,2,0:T(8,128)}, u32[]{:S(2)}) copy-start(f32[4,8,8,256]{3,1,2,0:T(8,128)} %copy.19) | copy-start | bytes 786436
  274.5 4.7 %copy-start.1 = (f32[2048,256]{1,0:T(8,128)S(1)}, f32[2048,256]{1,0:T(8,128)}, u32[]{:S(2)}) copy-start(f32[2048,256]{1,0:T(8,128)} %all-reduce.4.cloned.1.call-done) | copy-start | bytes 6291460
Sparse Core Ops, SparseCore 0:
  9.9 28.9 all-gather.1
  49.2 150.0 all-reduce.5
  206.3 68.1 all-reduce.3
where the time goes:
time: 431 us; the launch traced here: 430 us
  waiting for transfers between devices  221 us (51%)
  blocking collectives  143 us (33%)
  local copies, waits for them, and re-layouts  25.5 us (6%)
  matrix products  24.8 us (6%)
  between operations  13.9 us (3%)
    psum x1, waiting for transfers between devices, per_device(): lax.psum(stacked, 'row').astype(jnp.float32).astype(jnp.bfloat16)  150 us
    psum x1, blocking collectives, per_device(): grad_inverse = lax.psum(inverse_term, 'row')  143 us
    psum x1, waiting for transfers between devices, per_device(): grad_total = lax.psum(factor_grad, 'col')  46.6 us
    all_gather x1, waiting for transfers between devices, per_device(): gathered = lax.all_gather(panel_rows, 'col', axis=1, tiled=True)  24.5 us
    unnamed x15, local copies, waits for them, and re-layouts  15.7 us
  transfers between devices with their start and end apart: 3, of which 3 were waited for; matrix products, arithmetic and copies ran while one was open for 6% of the time, Pallas kernels for 0%

commit v1 on v0

--- a/solution.py
+++ b/solution.py
@@ -18,7 +18,8 @@
     highest = lax.Precision.HIGHEST
     contract_rows = (((0,), (0,)), ((), ()))
     panel_rows = panel.reshape(row_count, strip_width)
-    gathered = lax.all_gather(panel_rows, "col", axis=1, tiled=True)
+    outgoing = jnp.stack([panel_rows] * lax.axis_size("col"))
+    gathered = jnp.concatenate(lax.all_to_all(outgoing, "col", 0, 0), axis=1)
     factor = jnp.dot(gathered, inverse.T, precision=highest, preferred_element_type=jnp.float32)
     rounded = factor.astype(jnp.bfloat16)
     factor_tiles = rounded.reshape(tiles_local, tile_size, tile_size)

time: 431 us -> 431 us (level)
    all_gather x1 -> x0, waiting for transfers between devices: 24.5 us -> none  [per_device(): gathered = lax.all_gather(panel_rows, 'col', axis=1, tiled=True)]
    all_to_all x0 -> x1, waiting for transfers between devices: none -> 21.8 us  [per_device(): gathered = jnp.concatenate(lax.all_to_all(outgoing, 'col', 0, 0), axis=1)]
    unnamed x15 -> x17, local copies, waits for them, and re-layouts: 15.7 us -> 15 us
where the time goes in v1:
time: 431 us; the launch traced here: 430 us
  waiting for transfers between devices  218 us (51%)
  blocking collectives  143 us (33%)
  local copies, waits for them, and re-layouts  26.4 us (6%)
  matrix products  23.2 us (5%)
  between operations  14.2 us (3%)
    psum x1, waiting for transfers between devices, per_device(): lax.psum(stacked, 'row').astype(jnp.float32).astype(jnp.bfloat16)  150 us
    psum x1, blocking collectives, per_device(): grad_inverse = lax.psum(inverse_term, 'row')  143 us
    psum x1, waiting for transfers between devices, per_device(): grad_total = lax.psum(factor_grad, 'col')  46.5 us
    all_to_all x1, waiting for transfers between devices, per_device(): gathered = jnp.concatenate(lax.all_to_all(outgoing, 'col', 0, 0), axis=1)  21.8 us
    unnamed x17, local copies, waits for them, and re-layouts  15 us
  transfers between devices with their start and end apart: 3, of which 3 were waited for; matrix products, arithmetic and copies ran while one was open for 6% of the time, Pallas kernels for 0%

profile of v1, /device:TPU:0, one launch (start us, length us, event | category | flops | bytes accessed | tf_op | source)
XLA Modules:
  0.0 430.2 jit_solution(2429456965574969300)
XLA Ops:
  7.2 1.0 copy.19
  8.2 1.6 stack.4
  9.8 3.6 all-to-all-start
  13.5 5.2 %copy.20 = bf16[256,8,4,256]{3,1,2,0:T(8,128)(2,1)} copy(bf16[256,8,4,256]{3,2,1,0:T(4,128)(2,1)} %bitcast.75) | data formatting | bytes 8388608
  18.8 21.8 %all-to-all-done = f32[8,2048,32]{1,2,0:T(8,128)S(1)} async-done(((f32[8,2048,32]{1,2,0:T(8,128)}), f32[8,2048,32]{1,2,0:T(8,128)S(1)}, u32[]{:S(2)}, u32[]{:S(2)}) %all-to-all-start) | async-done | bytes 2097184 | tf_op jit(solution)/shard_map/all_to_all | solution.py:22
  40.5 3.4 convolution_convert_fusion
  44.0 4.3 fusion.1
  48.3 0.9 pad_maximum_fusion
  49.2 0.2 all-reduce.4.cloned.1.call-start
  49.4 149.8 %all-reduce.6.cloned.1.call-done = (bf16[1024,256]{1,0:T(8,128)(2,1)}, bf16[1024,256]{0,1:T(8,128)(2,1)}) async-done(((bf16[1024,256]{1,0:T(8,128)(2,1)}, bf16[1024,256]{0,1:T(8,128)(2,1)}), (bf16[1024,256]{1,0:T(8,128)(2,1)}, bf16[1024,256]{0,1:T(8,128)(2,1)})) %all-reduce.6.cloned.1.call-update) | async-done | bytes 1048592 | tf_op jit(solution)/shard_map/psum | solution.py:35
  199.2 3.7 convolution_negate_fusion
  202.9 0.2 copy.24
  203.1 0.9 copy-done.5
  203.9 0.1 convert_element_type.29
  204.3 1.8 copy.14
  206.2 7.0 %copy.18 = f32[256,8,4,256]{3,1,2,0:T(8,128)} copy(bf16[256,8,4,256]{3,2,1,0:T(4,128)(2,1)} %bitcast.74) | data formatting | bytes 12582912
  213.2 6.8 %subtract_convert_fusion = bf16[2048,1024]{1,0:T(8,128)(2,1)} fusion(f32[2048,1024]{1,0:T(8,128)} %bitcast.69, bf16[2048,256]{1,0:T(8,128)(2,1)S(1)} %convolution_convert_fusion, bf16[1024,256]{1,0:T(8,128)(2,1)S(1)} %copy-done.4), kind=kOutput, calls=%fused_computation | convolution fusion | flops 1077936128 | bytes 14155776 | tf_op jit(solution)/shard_map/dot_general | solution.py:37
  220.0 7.9 %reshape.43 = bf16[8,1,256,4,1,256]{5,3,2,0,4,1:T(4,128)(2,1)} reshape(bf16[2048,1024]{1,0:T(8,128)(2,1)} %subtract_convert_fusion) | data formatting | bytes 8388608 | tf_op jit(solution)/shard_map/reshape | solution.py:67
  227.9 46.5 %all-reduce.4.cloned.1.call-done = f32[2048,256]{1,0:T(8,128)} async-done(((f32[2048,256]{1,0:T(8,128)}), f32[2048,256]{1,0:T(8,128)}) %all-reduce.4.cloned.1.call-update) | async-done | bytes 2097168 | tf_op jit(solution)/shard_map/psum | solution.py:58
  274.4 3.8 fusion.14
  278.2 0.1 copy.21
  278.3 0.8 copy.16
  279.1 1.2 fusion.17
  280.2 143.1 %psum.31 = f32[256,32]{0,1:T(8,128)} all-reduce(f32[256,32]{0,1:T(8,128)S(1)} %fusion.17), channel_id=1, replica_groups=mesh['row'=32,'col'=8] {'row'}, use_global_device_ids=true, to_apply=%region_3.4 | all-reduce | flops 8192 | bytes 65536 | tf_op jit(solution)/shard_map/psum | solution.py:66
  (19 shorter events, 0.4 us)
Async XLA Ops:
  7.2 33.4 %copy-start = (f32[256,256]{1,0:T(8,128)S(1)}, f32[256,256]{1,0:T(8,128)}, u32[]{:S(2)}) copy-start(f32[256,256]{1,0:T(8,128)} %param.7) | copy-start | bytes 786436
  8.2 1.6 copy-start.2
  9.8 30.7 %all-to-all-start = ((f32[8,2048,32]{1,2,0:T(8,128)}), f32[8,2048,32]{1,2,0:T(8,128)S(1)}, u32[]{:S(2)}, u32[]{:S(2)}) async-start(f32[8,2048,32]{1,2,0:T(8,128)} %stack.4), calls=%async_computation | async-start | bytes 4194304 | tf_op jit(solution)/shard_map/all_to_all | solution.py:22
  13.4 185.8 %all-reduce.6.cloned.1.call-start = ((), (), s32[]{:S(2)}) async-start(), calls=%async_computation.2 | async-start | bytes 2097152 | tf_op jit(solution)/shard_map/psum | solution.py:35
  49.2 225.2 %all-reduce.4.cloned.1.call-start = ((), (), s32[]{:S(2)}) async-start(), calls=%async_computation.1 | async-start | bytes 4194304 | tf_op jit(solution)/shard_map/psum | solution.py:58
  202.9 1.0 copy-start.5
  206.1 7.0 %copy-start.4 = (bf16[1024,256]{1,0:T(8,128)(2,1)S(1)}, bf16[1024,256]{1,0:T(8,128)(2,1)}, u32[]{:S(2)}) copy-start(bf16[1024,256]{1,0:T(8,128)(2,1)} %get-tuple-element.9) | copy-start | bytes 1572868
  227.9 51.2 %copy-start.3 = (f32[4,8,8,256]{3,1,2,0:T(8,128)S(1)}, f32[4,8,8,256]{3,1,2,0:T(8,128)}, u32[]{:S(2)}) copy-start(f32[4,8,8,256]{3,1,2,0:T(8,128)} %copy-done.2) | copy-start | bytes 786436
  274.4 4.7 %copy-start.1 = (f32[2048,256]{1,0:T(8,128)S(1)}, f32[2048,256]{1,0:T(8,128)}, u32[]{:S(2)}) copy-start(f32[2048,256]{1,0:T(8,128)} %all-reduce.4.cloned.1.call-done) | copy-start | bytes 6291460
Sparse Core Ops, SparseCore 0:
  49.3 149.8 all-reduce.5
  206.3 68.0 all-reduce.3
